TPU v7x, 128 devices: a whole 4x4x4 slice. The times are simulated.
128 devices in a mesh: replica: 4 (over z), shard: 16 (over y, x_lo, core), tensor: 2 (over x_hi).
Axes of the slice: x: 4 (x_hi: 2, x_lo: 2; x = x_hi * 2 + x_lo), y: 4, z: 4, core: 2. Of those that a mesh axis runs over, the one named last changes fastest.
Arguments:
- trained_up: bfloat16 [4, 1024, 4096], P('replica', None, 'tensor'), may hold values from -6 to 6
- trained_down: bfloat16 [4, 4096, 1024], P('replica', 'tensor'), may hold values from -6 to 6
- trained_embed: bfloat16 [4, 32768, 1024], P('replica', ('shard', 'tensor')), may hold values from -6 to 6
- trained_norm: bfloat16 [4, 2, 1024], P('replica'), may hold values from 0.099609375 to 1.8984375
- master_up: float32 [1024, 4096], P(('replica', 'shard', 'tensor')), may hold values from -6 to 6
- moment_up: float32 [1024, 4096], P(('replica', 'shard', 'tensor')), may hold values from -4 to 4
- master_down: float32 [2, 2048, 1024], P('tensor', ('replica', 'shard')), may hold values from -6 to 6
- moment_down: float32 [2, 2048, 1024], P('tensor', ('replica', 'shard')), may hold values from -4 to 4
- master_embed: float32 [32, 1024, 1024], P(('shard', 'tensor'), 'replica'), may hold values from -6 to 6
- moment_embed: float32 [32, 1024, 64], P(('shard', 'tensor'), 'replica'), may hold values from -4 to 4
- master_norm: float32 [2, 1024], replicated, may hold values from 0.1 to 1.9
- moment_norm: float32 [2, 1024], replicated, may hold values from -2 to 2
- embed_basis: float32 [1024, 64], replicated, may hold values from -0.1875 to 0.1875
Outputs:
- recast_up: bfloat16 [1024, 4096], P(None, 'tensor')
- recast_down: bfloat16 [4096, 1024], P('tensor')
- recast_embed: bfloat16 [32768, 1024], P(('shard', 'tensor'))
- recast_norm: bfloat16 [2, 1024], replicated
- stored_up: float32 [1024, 4096], P(('replica', 'shard', 'tensor'))
- velocity_up: float32 [1024, 4096], P(('replica', 'shard', 'tensor'))
- stored_down: float32 [2, 2048, 1024], P('tensor', ('replica', 'shard'))
- velocity_down: float32 [2, 2048, 1024], P('tensor', ('replica', 'shard'))
- stored_embed: float32 [32, 1024, 1024], P(('shard', 'tensor'), 'replica')
- velocity_embed: float32 [32, 1024, 64], P(('shard', 'tensor'), 'replica')
- stored_norm: float32 [2, 1024], replicated
- velocity_norm: float32 [2, 1024], replicated
All inputs are finite; a program needn't handle non-finite values.
Results may differ from a plain program's by a relative error of at most 0.012.
Values may be sent and summed in bfloat16 or wider, within the bound.
A program may use at most 128 MiB of HBM per device.

v0:
```python
import jax
import jax.numpy as jnp
from jax import lax
from jax.sharding import PartitionSpec as P


def outer_step(master, moment, summed, groups):
    difference = master - summed / groups
    velocity = 0.5 * moment + difference
    return (master - 0.7 * (difference + 0.5 * velocity), velocity)


def body(
    trained_up,
    trained_down,
    trained_embed,
    trained_norm,
    master_up,
    moment_up,
    master_down,
    moment_down,
    master_embed,
    moment_embed,
    master_norm,
    moment_norm,
    embed_basis,
):
    replicas = lax.axis_size("replica")
    shards = lax.axis_size("shard")
    tensors = lax.axis_size("tensor")
    shard_pos = lax.axis_index("shard")
    width = embed_basis.shape[0]
    rows_up = master_up.shape[0]
    half_cols = trained_up.shape[2]
    rows_down = master_down.shape[1]
    up_blocks = trained_up[0].reshape(replicas, shards, tensors, rows_up, half_cols)
    up_own = lax.dynamic_index_in_dim(up_blocks, shard_pos, 1, keepdims=False)
    down_blocks = trained_down[0].reshape(replicas, shards, rows_down, width)
    down_own = lax.dynamic_index_in_dim(down_blocks, shard_pos, 1, keepdims=False)
    up_summed, down_summed = (
        lax.psum_scatter(
            up_own.astype(jnp.float32).astype(jnp.bfloat16),
            "replica",
            scatter_dimension=0,
            tiled=True,
        ).astype(jnp.float32),
        lax.psum_scatter(
            down_own.astype(jnp.float32).astype(jnp.bfloat16),
            "replica",
            scatter_dimension=0,
            tiled=True,
        ).astype(jnp.float32),
    )
    up_summed = lax.all_to_all(up_summed, "tensor", split_axis=1, concat_axis=3, tiled=True)
    stored_up, velocity_up = outer_step(
        master_up, moment_up, up_summed.reshape(rows_up, half_cols * tensors), replicas
    )
    stored_down, velocity_down = outer_step(master_down, moment_down, down_summed, replicas)
    norm_summed = lax.psum(trained_norm[0].astype(jnp.float32), "replica")
    stored_norm, velocity_norm = outer_step(master_norm, moment_norm, norm_summed, replicas)
    embed_own = master_embed[0]
    rows_embed = embed_own.shape[0]
    embed_terms = trained_embed[0].reshape(replicas, rows_embed, width).astype(jnp.float32)
    embed_summed = lax.psum_scatter(
        embed_terms.astype(jnp.bfloat16), "replica", scatter_dimension=0, tiled=True
    ).astype(jnp.float32)[0]
    coefficient = jnp.dot(
        embed_own - embed_summed / replicas, embed_basis, precision=lax.Precision.HIGHEST
    )
    velocity_rows = 0.5 * moment_embed[0] + coefficient
    stored_rows = embed_own - 0.7 * jnp.dot(
        coefficient + 0.5 * velocity_rows, embed_basis.T, precision=lax.Precision.HIGHEST
    )
    up_piece = lax.all_to_all(
        stored_up.astype(jnp.bfloat16), "tensor", split_axis=1, concat_axis=0, tiled=True
    )
    down_piece = stored_down[0].astype(jnp.bfloat16)
    recast_up, recast_down = (
        lax.all_gather(up_piece, ("replica", "shard"), axis=0, tiled=True),
        lax.all_gather(down_piece, ("replica", "shard"), axis=0, tiled=True),
    )
    recast_embed = lax.all_gather(stored_rows.astype(jnp.bfloat16), "replica", axis=0, tiled=True)
    return (
        recast_up,
        recast_down,
        recast_embed,
        stored_norm.astype(jnp.bfloat16),
        stored_up,
        velocity_up,
        stored_down,
        velocity_down,
        stored_rows[None],
        velocity_rows[None],
        stored_norm,
        velocity_norm,
    )


def solution(mesh):
    in_specs = (
        P("replica", None, "tensor"),
        P("replica", "tensor", None),
        P("replica", ("shard", "tensor"), None),
        P("replica", None, None),
        P(("replica", "shard", "tensor"), None),
        P(("replica", "shard", "tensor"), None),
        P("tensor", ("replica", "shard"), None),
        P("tensor", ("replica", "shard"), None),
        P(("shard", "tensor"), "replica", None),
        P(("shard", "tensor"), "replica", None),
        P(),
        P(),
        P(),
    )
    out_specs = (
        P(None, "tensor"),
        P("tensor", None),
        P(("shard", "tensor"), None),
        P(),
        P(("replica", "shard", "tensor"), None),
        P(("replica", "shard", "tensor"), None),
        P("tensor", ("replica", "shard"), None),
        P("tensor", ("replica", "shard"), None),
        P(("shard", "tensor"), "replica", None),
        P(("shard", "tensor"), "replica", None),
        P(),
        P(),
    )
    return jax.shard_map(body, mesh=mesh, in_specs=in_specs, out_specs=out_specs, check_vma=False)
```

profile of v0, /device:TPU:1, one launch (start us, length us, event | category | flops | bytes accessed | tf_op | source)
XLA Modules:
  0.0 376.6 jit_solution(8853071086595991756)
XLA Ops:
  7.2 0.0 copy-start
  7.2 0.0 copy-start.1
  7.2 0.0 copy-start.4
  7.2 0.0 reduce-scatter.6.cloned.1.call-start
  7.3 0.0 copy-start.12
  7.3 0.7 reduce-scatter.6.cloned.1.call-update
  7.9 0.0 copy-start.7
  8.0 0.0 copy-start.8
  8.0 0.0 all-reduce.3.cloned.1.call-start
  8.0 1.7 copy_bitcast_fusion
  9.7 0.0 all-reduce.3.cloned.1.call-update
  9.7 0.0 reduce-scatter.4.cloned.1.call-start
  9.8 0.0 copy-start.11
  9.8 1.7 dynamic-slice_bitcast_fusion
  11.5 0.0 reduce-scatter.4.cloned.1.call-update
  11.5 0.0 all-gather.7.cloned.1.call-start
  11.6 32.1 %reduce-scatter.6.cloned.1.call-done = bf16[1,256,1024]{2,1,0:T(8,128)(2,1)} async-done(((bf16[4,256,1024]{2,1,0:T(8,128)(2,1)}), bf16[1,256,1024]{2,1,0:T(8,128)(2,1)}) %reduce-scatter.6.cloned.1.call-update) | async-done | bytes 524304 | tf_op jit(solution)/shard_map/reduce_scatter | solution.py:64
  43.6 0.0 copy-done
  43.6 0.0 copy-done.1
  43.6 2.2 fusion.1
  45.8 0.0 copy-done.4
  45.8 2.2 fusion.16
  48.0 0.0 all-gather.7.cloned.1.call-update
  48.1 0.0 all-gather.5.cloned.1.call-start
  48.1 0.0 copy-done.12
  48.1 0.6 dynamic-slice
  48.7 37.3 %all-reduce.3.cloned.1.call-done = bf16[4,2,8,2048]{3,2,0,1:T(8,128)(2,1)} async-done(((bf16[4,2,8,2048]{3,2,0,1:T(8,128)(2,1)}), bf16[4,2,8,2048]{3,2,0,1:T(8,128)(2,1)}) %all-reduce.3.cloned.1.call-update) | async-done | bytes 262160
  86.0 1.5 dynamic-slice_convert_fusion
  87.5 8.6 %all_to_all.28 = f32[1,2,8,2048]{3,2,0,1:T(8,128)S(1)} all-to-all(f32[1,2,8,2048]{3,2,0,1:T(8,128)S(1)} %dynamic-slice_convert_fusion), channel_id=1, replica_groups=mesh['replica'=4,'shard'=16,'tensor'=2] {'tensor'}, dimensions={1} | all-to-all | bytes 262144 | tf_op jit(solution)/shard_map/all_to_all | solution.py:54
  96.1 0.7 fusion.15
  96.9 7.5 %all_to_all.29 = bf16[8,2,2048]{2,0,1:T(8,128)(2,1)} all-to-all(bf16[8,2,2048]{2,0,1:T(8,128)(2,1)S(1)} %bitcast.53), channel_id=1, replica_groups=mesh['replica'=4,'shard'=16,'tensor'=2] {'tensor'}, dimensions={1} | all-to-all | bytes 131072 | tf_op jit(solution)/shard_map/all_to_all | solution.py:74
  104.4 0.0 all-gather.5.cloned.1.call-update
  104.4 0.0 all-gather.9.cloned.1.call-start
  104.4 5.8 %reduce-scatter.4.cloned.1.call-done = bf16[1,32,1024]{2,1,0:T(8,128)(2,1)} async-done(((bf16[4,32,1024]{2,1,0:T(8,128)(2,1)}), bf16[1,32,1024]{2,1,0:T(8,128)(2,1)}) %reduce-scatter.4.cloned.1.call-update) | async-done | bytes 65552 | tf_op jit(solution)/shard_map/reduce_scatter | solution.py:47
  110.3 0.0 copy-done.6
  110.3 1.6 fusion.14
  111.9 0.0 all-gather.9.cloned.1.call-update
  111.9 6.9 %psum.7 = f32[2,1024]{1,0:T(2,128)S(1)} all-reduce(f32[2,1024]{1,0:T(2,128)S(1)} %bitcast_convert_fusion), channel_id=1, replica_groups=mesh['replica'=4,'shard'=16,'tensor'=2] {'replica'}, use_global_device_ids=true, to_apply=%region_3.4 | all-reduce | flops 2048 | bytes 16384 | tf_op jit(solution)/shard_map/psum | solution.py:59
  118.9 0.6 fusion.13
  119.5 0.6 fusion.8
  120.2 25.0 %all-gather.7.cloned.1.call-done = bf16[1024,1024]{1,0:T(8,128)(2,1)} async-done(((bf16[256,1024]{1,0:T(8,128)(2,1)}), bf16[1024,1024]{1,0:T(8,128)(2,1)}) %all-gather.7.cloned.1.call-update) | async-done | bytes 2097168 | tf_op jit(solution)/shard_map/all_gather | solution.py:82
  145.2 108.0 %all-gather.5.cloned.1.call-done = bf16[1024,2048]{1,0:T(8,128)(2,1)} async-done(((bf16[16,2048]{1,0:T(8,128)(2,1)}), bf16[1024,2048]{1,0:T(8,128)(2,1)}) %all-gather.5.cloned.1.call-update) | async-done | bytes 4194320 | tf_op jit(solution)/shard_map/all_gather | solution.py:79
  253.2 107.3 %all-gather.9.cloned.1.call-done = bf16[1,2048,1024]{2,1,0:T(8,128)(2,1)} async-done(((bf16[1,32,1024]{2,1,0:T(8,128)(2,1)}), bf16[1,2048,1024]{2,1,0:T(8,128)(2,1)}) %all-gather.9.cloned.1.call-update) | async-done | bytes 4194320 | tf_op jit(solution)/shard_map/all_gather | solution.py:80
  360.4 4.9 %copy.39 = bf16[1024,2048]{1,0:T(8,128)(2,1)} copy(bf16[1024,2048]{1,0:T(8,128)(2,1)} %all-gather.5.cloned.1.call-done) | data formatting | bytes 8388608
  365.4 0.0 copy-done.2
  365.4 2.1 copy.40
  367.5 1.0 copy-done.3
  368.5 1.3 copy.41
  (14 shorter events, 0.0 us)
Async XLA Ops:
  7.2 36.5 %copy-start = (f32[1024,64]{0,1:T(8,128)S(1)}, f32[1024,64]{0,1:T(8,128)}, u32[]{:S(2)}) copy-start(f32[1024,64]{0,1:T(8,128)} %param.25) | copy-start | bytes 786436
  7.2 36.5 %copy-start.1 = (f32[1,256,1024]{2,1,0:T(8,128)S(1)}, f32[1,256,1024]{2,1,0:T(8,128)}, u32[]{:S(2)}) copy-start(f32[1,256,1024]{2,1,0:T(8,128)} %param.21) | copy-start | bytes 3145732
  7.2 38.6 %copy-start.4 = (f32[1,256,64]{1,2,0:T(8,128)S(1)}, f32[1,256,64]{1,2,0:T(8,128)}, u32[]{:S(2)}) copy-start(f32[1,256,64]{1,2,0:T(8,128)} %param.22) | copy-start | bytes 196612
  7.2 36.4 %reduce-scatter.6.cloned.1.call-start = ((), (), s32[]{:S(2)}) async-start(), calls=%async_computation.6 | async-start | bytes 2621440 | tf_op jit(solution)/shard_map/reduce_scatter | solution.py:64
  7.3 40.9 %copy-start.12 = (u32[128]{0:T(128)S(1)}, u32[128]{0:T(128)}, u32[]{:S(2)}) copy-start(u32[128]{0:T(128)} %constant.47) | copy-start | bytes 1540
  7.9 88.2 %copy-start.7 = (f32[8,4096]{1,0:T(8,128)S(1)}, f32[8,4096]{1,0:T(8,128)}, u32[]{:S(2)}) copy-start(f32[8,4096]{1,0:T(8,128)} %param.17) | copy-start | bytes 393220
  8.0 88.2 %copy-start.8 = (f32[8,4096]{1,0:T(8,128)S(1)}, f32[8,4096]{1,0:T(8,128)}, u32[]{:S(2)}) copy-start(f32[8,4096]{1,0:T(8,128)} %param.18) | copy-start | bytes 393220
  8.0 78.0 %all-reduce.3.cloned.1.call-start = ((), (), s32[]{:S(2)}) async-start(), calls=%async_computation.9 | async-start | bytes 524288
  9.7 100.6 %copy-start.5 = (f32[1,32,1024]{2,1,0:T(8,128)S(1)}, f32[1,32,1024]{2,1,0:T(8,128)}, u32[]{:S(2)}) copy-start(f32[1,32,1024]{2,1,0:T(8,128)} %param.19) | copy-start | bytes 393220
  9.7 100.6 %copy-start.6 = (f32[1,32,1024]{2,1,0:T(8,128)S(1)}, f32[1,32,1024]{2,1,0:T(8,128)}, u32[]{:S(2)}) copy-start(f32[1,32,1024]{2,1,0:T(8,128)} %param.20) | copy-start | bytes 393220
  9.7 100.6 %reduce-scatter.4.cloned.1.call-start = ((), (), s32[]{:S(2)}) async-start(), calls=%async_computation.5 | async-start | bytes 327680 | tf_op jit(solution)/shard_map/reduce_scatter | solution.py:47
  9.8 102.1 %copy-start.11 = (bf16[1,2,1024]{2,1,0:T(2,128)(2,1)S(1)}, bf16[1,2,1024]{2,1,0:T(2,128)(2,1)}, u32[]{:S(2)}) copy-start(bf16[1,2,1024]{2,1,0:T(2,128)(2,1)} %param.16) | copy-start | bytes 12292
  11.5 107.4 %copy-start.9 = (f32[2,1024]{1,0:T(2,128)S(1)}, f32[2,1024]{1,0:T(2,128)}, u32[]{:S(2)}) copy-start(f32[2,1024]{1,0:T(2,128)} %param.23) | copy-start | bytes 24580
  11.5 107.4 %copy-start.10 = (f32[2,1024]{1,0:T(2,128)S(1)}, f32[2,1024]{1,0:T(2,128)}, u32[]{:S(2)}) copy-start(f32[2,1024]{1,0:T(2,128)} %param.24) | copy-start | bytes 24580
  11.5 133.6 %all-gather.7.cloned.1.call-start = ((), (), s32[]{:S(2)}) async-start(), calls=%async_computation.7 | async-start | bytes 2621440 | tf_op jit(solution)/shard_map/all_gather | solution.py:82
  48.1 205.1 %all-gather.5.cloned.1.call-start = ((), (), s32[]{:S(2)}) async-start(), calls=%async_computation.4 | async-start | bytes 4259840 | tf_op jit(solution)/shard_map/all_gather | solution.py:79
  104.4 256.0 %all-gather.9.cloned.1.call-start = ((), (), s32[]{:S(2)}) async-start(), calls=%async_computation.8 | async-start | bytes 4259840 | tf_op jit(solution)/shard_map/all_gather | solution.py:80
  360.4 4.9 %copy-start.2 = (bf16[1,2048,1024]{2,1,0:T(8,128)(2,1)S(1)}, bf16[1,2048,1024]{2,1,0:T(8,128)(2,1)}, u32[]{:S(2)}) copy-start(bf16[1,2048,1024]{2,1,0:T(8,128)(2,1)} %all-gather.9.cloned.1.call-done) | copy-start | bytes 12582916
  365.4 3.1 copy-start.3
Sparse Core Ops, SparseCore 0:
  10.4 33.1 reduce-scatter.5
  46.7 39.3 all-reduce.2
  89.0 21.2 reduce-scatter.3
  112.5 32.6 all-gather.6
  146.9 106.2 all-gather.4
  255.4 104.9 all-gather.8
where the time goes:
time: 377 us
  waiting for transfers between devices  316 us (84%)
  blocking collectives  23 us (6%)
  between operations  14.3 us (4%)
  local copies, waits for them, and re-layouts  13.4 us (4%)
  other arithmetic  5.09 us (1%)
  matrix products  4.38 us (1%)
    all_gather x1, waiting for transfers between devices, body(): lax.all_gather(up_piece, ('replica', 'shard'), axis=0, tiled=True)  108 us
    all_gather x1, waiting for transfers between devices, body(): lax.all_gather(down_piece, ('replica', 'shard'), axis=0, tiled=True)  107 us
    unnamed x7, waiting for transfers between devices  38.1 us
    reduce_scatter x1, waiting for transfers between devices, body(): lax.psum_scatter(embed_terms.astype(jnp.bfloat16), 'replica', scatter_dim...  32.1 us
    all_gather x1, waiting for transfers between devices, body(): lax.all_gather(stored_rows.astype(jnp.bfloat16), 'replica', axis=0, tiled...  25 us
    unnamed x30, local copies, waits for them, and re-layouts  10 us
    all_to_all x1, blocking collectives, body(): lax.all_to_all(up_summed, 'tensor', split_axis=1, concat_axis=3, tiled=True)  8.59 us
  transfers between devices with their start and end apart: 6, of which 6 were waited for; matrix products, arithmetic and copies ran while one was open for 4% of the time, Pallas kernels for 0%

commit v1 on v0

--- a/solution.py
+++ b/solution.py
@@ -2,6 +2,11 @@
 import jax.numpy as jnp
 from jax import lax
 from jax.sharding import PartitionSpec as P
+
+
+def gather_from_all(x, axis, dim):
+    copies = jnp.concatenate([x] * lax.axis_size(axis), axis=dim)
+    return lax.all_to_all(copies, axis, dim, dim, tiled=True)
 
 
 def outer_step(master, moment, summed, groups):
@@ -79,7 +84,7 @@
         lax.all_gather(up_piece, ("replica", "shard"), axis=0, tiled=True),
         lax.all_gather(down_piece, ("replica", "shard"), axis=0, tiled=True),
     )
-    recast_embed = lax.all_gather(stored_rows.astype(jnp.bfloat16), "replica", axis=0, tiled=True)
+    recast_embed = gather_from_all(stored_rows.astype(jnp.bfloat16), "replica", 0)
     return (
         recast_up,
         recast_down,

time: 377 us -> 353 us (0.936)
  waiting for transfers between devices: 316 us -> 261 us
  blocking collectives: 23 us -> 50.1 us
    all_gather x1, waiting for transfers between devices: 108 us -> 73.4 us  [body(): lax.all_gather(up_piece, ('replica', 'shard'), axis=0, tiled=True)]
    psum x1, blocking collectives: 6.93 us -> 34 us  [body(): norm_summed = lax.psum(trained_norm[0].astype(jnp.float32), 'replica')]
    all_gather x1 -> x0, waiting for transfers between devices: 25 us -> none  [body(): lax.all_gather(stored_rows.astype(jnp.bfloat16), 'replica', axis=0, tiled...]
    unnamed x7 -> x6, waiting for transfers between devices: 38.1 us -> 41.8 us
    unnamed x30 -> x26, local copies, waits for them, and re-layouts: 10 us -> 9.57 us
  transfers between devices with their start and end apart: 6 -> 6, of which waited for: 6 -> 5; matrix products, arithmetic and copies ran while one was open for 4% -> 4% of each run, Pallas kernels for 0% -> 0%
where the time goes in v1:
time: 353 us
  waiting for transfers between devices  261 us (74%)
  blocking collectives  50.1 us (14%)
  between operations  14 us (4%)
  local copies, waits for them, and re-layouts  13.1 us (4%)
  other arithmetic  6.69 us (2%)
  matrix products  4.21 us (1%)
  starting transfers between devices  3.81 us (1%)
    all_gather x1, waiting for transfers between devices, body(): lax.all_gather(down_piece, ('replica', 'shard'), axis=0, tiled=True)  107 us
    all_gather x1, waiting for transfers between devices, body(): lax.all_gather(up_piece, ('replica', 'shard'), axis=0, tiled=True)  73.4 us
    unnamed x6, waiting for transfers between devices  41.8 us
    psum x1, blocking collectives, body(): norm_summed = lax.psum(trained_norm[0].astype(jnp.float32), 'replica')  34 us
    reduce_scatter x1, waiting for transfers between devices, body(): lax.psum_scatter(embed_terms.astype(jnp.bfloat16), 'replica', scatter_dim...  32.4 us
    unnamed x26, local copies, waits for them, and re-layouts  9.57 us
    all_to_all x1, blocking collectives, body(): lax.all_to_all(up_summed, 'tensor', split_axis=1, concat_axis=3, tiled=True)  8.59 us
    all_to_all x1, blocking collectives, body(): lax.all_to_all(stored_up.astype(jnp.bfloat16), 'tensor', split_axis=1, co...  7.5 us
  transfers between devices with their start and end apart: 6, of which 5 were waited for; matrix products, arithmetic and copies ran while one was open for 4% of the time, Pallas kernels for 0%

profile of v1, /device:TPU:1, one launch (start us, length us, event | category | flops | bytes accessed | tf_op | source)
XLA Modules:
  0.0 352.7 jit_solution(13000381479985502903)
XLA Ops:
  7.2 0.0 copy-start
  7.2 0.0 copy-start.6
  7.2 0.0 copy-start.7
  7.2 0.0 copy-start.4
  7.2 0.0 copy-start.5
  7.2 0.0 copy-start.1
  7.2 0.0 copy-start.3
  7.3 0.0 all-reduce.3.cloned.1.call-start
  7.3 1.8 copy_bitcast_fusion
  9.1 0.0 all-reduce.3.cloned.1.call-update
  9.2 0.0 reduce-scatter.4.cloned.1.call-start
  9.2 1.7 dynamic-slice_bitcast_fusion
  10.9 0.0 reduce-scatter.4.cloned.1.call-update
  10.9 0.0 reduce-scatter.6.cloned.1.call-start
  11.0 0.7 reduce-scatter.6.cloned.1.call-update
  11.6 0.0 all-gather.4.cloned.1.call-start
  11.7 1.2 dynamic-slice
  12.9 41.1 %all-reduce.3.cloned.1.call-done = bf16[4,2,8,2048]{3,2,0,1:T(8,128)(2,1)} async-done(((bf16[4,2,8,2048]{3,2,0,1:T(8,128)(2,1)}), bf16[4,2,8,2048]{3,2,0,1:T(8,128)(2,1)}) %all-reduce.3.cloned.1.call-update) | async-done | bytes 262160
  54.0 1.5 dynamic-slice_convert_fusion
  55.5 8.6 %all_to_all.40 = f32[1,2,8,2048]{3,2,0,1:T(8,128)S(1)} all-to-all(f32[1,2,8,2048]{3,2,0,1:T(8,128)S(1)} %dynamic-slice_convert_fusion), channel_id=1, replica_groups=mesh['replica'=4,'shard'=16,'tensor'=2] {'tensor'}, dimensions={1} | all-to-all | bytes 262144 | tf_op jit(solution)/shard_map/all_to_all | solution.py:59
  64.1 0.0 copy-done.6
  64.1 0.0 copy-done.7
  64.2 0.7 fusion.15
  64.9 7.5 %all_to_all.41 = bf16[8,2,2048]{2,0,1:T(8,128)(2,1)} all-to-all(bf16[8,2,2048]{2,0,1:T(8,128)(2,1)S(1)} %bitcast.56), channel_id=1, replica_groups=mesh['replica'=4,'shard'=16,'tensor'=2] {'tensor'}, dimensions={1} | all-to-all | bytes 131072 | tf_op jit(solution)/shard_map/all_to_all | solution.py:79
  72.4 0.0 all-gather.4.cloned.1.call-update
  72.4 0.0 all-gather.6.cloned.1.call-start
  72.5 6.0 %reduce-scatter.4.cloned.1.call-done = bf16[1,32,1024]{2,1,0:T(8,128)(2,1)} async-done(((bf16[4,32,1024]{2,1,0:T(8,128)(2,1)}), bf16[1,32,1024]{2,1,0:T(8,128)(2,1)}) %reduce-scatter.4.cloned.1.call-update) | async-done | bytes 65552 | tf_op jit(solution)/shard_map/reduce_scatter | solution.py:52
  78.4 0.0 copy-done.4
  78.4 0.0 copy-done.5
  78.4 1.6 fusion.14
  80.0 0.0 all-gather.6.cloned.1.call-update
  80.1 32.4 %reduce-scatter.6.cloned.1.call-done = bf16[1,256,1024]{2,1,0:T(8,128)(2,1)} async-done(((bf16[4,256,1024]{2,1,0:T(8,128)(2,1)}), bf16[1,256,1024]{2,1,0:T(8,128)(2,1)}) %reduce-scatter.6.cloned.1.call-update) | async-done | bytes 524304 | tf_op jit(solution)/shard_map/reduce_scatter | solution.py:69
  112.4 0.0 copy-done.1
  112.4 2.2 fusion.1
  114.6 0.0 copy-start.8
  114.6 0.0 copy-start.9
  114.6 2.0 fusion.16
  116.7 1.6 pad_maximum_fusion
  118.3 3.6 %all-to-all-start.2 = ((bf16[4,256,1024]{2,1,0:T(8,128)(2,1)}), bf16[4,256,1024]{2,1,0:T(8,128)(2,1)S(1)}, u32[]{:S(2)}, u32[]{:S(2)}) async-start(bf16[4,256,1024]{2,1,0:T(8,128)(2,1)} %bitcast.15), calls=%async_computation.4 | async-start | bytes 4194304 | tf_op jit(solution)/shard_map/all_to_all | solution.py:9
  121.9 34.0 %psum.7 = f32[2,1024]{1,0:T(2,128)S(1)} all-reduce(f32[2,1024]{1,0:T(2,128)S(1)} %bitcast_convert_fusion), channel_id=1, replica_groups=mesh['replica'=4,'shard'=16,'tensor'=2] {'replica'}, use_global_device_ids=true, to_apply=%region_3.4 | all-reduce | flops 2048 | bytes 16384 | tf_op jit(solution)/shard_map/psum | solution.py:64
  155.9 0.6 fusion.13
  156.5 0.6 fusion.8
  157.2 0.0 all-to-all-done.2
  157.2 73.4 %all-gather.4.cloned.1.call-done = bf16[1024,2048]{1,0:T(8,128)(2,1)} async-done(((bf16[16,2048]{1,0:T(8,128)(2,1)}), bf16[1024,2048]{1,0:T(8,128)(2,1)}) %all-gather.4.cloned.1.call-update) | async-done | bytes 4194320 | tf_op jit(solution)/shard_map/all_gather | solution.py:84
  230.6 107.4 %all-gather.6.cloned.1.call-done = bf16[1,2048,1024]{2,1,0:T(8,128)(2,1)} async-done(((bf16[1,32,1024]{2,1,0:T(8,128)(2,1)}), bf16[1,2048,1024]{2,1,0:T(8,128)(2,1)}) %all-gather.6.cloned.1.call-update) | async-done | bytes 4194320 | tf_op jit(solution)/shard_map/all_gather | solution.py:85
  337.9 4.9 %copy.39 = bf16[1024,2048]{1,0:T(8,128)(2,1)} copy(bf16[1024,2048]{1,0:T(8,128)(2,1)} %all-gather.4.cloned.1.call-done) | data formatting | bytes 8388608
  342.9 2.0 copy.40
  344.9 1.3 copy.41
  (10 shorter events, 0.0 us)
Async XLA Ops:
  7.2 105.3 %copy-start = (f32[1024,64]{0,1:T(8,128)S(1)}, f32[1024,64]{0,1:T(8,128)}, u32[]{:S(2)}) copy-start(f32[1024,64]{0,1:T(8,128)} %param.25) | copy-start | bytes 786436
  7.2 56.9 %copy-start.6 = (f32[8,4096]{1,0:T(8,128)S(1)}, f32[8,4096]{1,0:T(8,128)}, u32[]{:S(2)}) copy-start(f32[8,4096]{1,0:T(8,128)} %param.17) | copy-start | bytes 393220
  7.2 56.9 %copy-start.7 = (f32[8,4096]{1,0:T(8,128)S(1)}, f32[8,4096]{1,0:T(8,128)}, u32[]{:S(2)}) copy-start(f32[8,4096]{1,0:T(8,128)} %param.18) | copy-start | bytes 393220
  7.2 71.2 %copy-start.4 = (f32[1,32,1024]{2,1,0:T(8,128)S(1)}, f32[1,32,1024]{2,1,0:T(8,128)}, u32[]{:S(2)}) copy-start(f32[1,32,1024]{2,1,0:T(8,128)} %param.19) | copy-start | bytes 393220
  7.2 71.2 %copy-start.5 = (f32[1,32,1024]{2,1,0:T(8,128)S(1)}, f32[1,32,1024]{2,1,0:T(8,128)}, u32[]{:S(2)}) copy-start(f32[1,32,1024]{2,1,0:T(8,128)} %param.20) | copy-start | bytes 393220
  7.2 105.2 %copy-start.1 = (f32[1,256,1024]{2,1,0:T(8,128)S(1)}, f32[1,256,1024]{2,1,0:T(8,128)}, u32[]{:S(2)}) copy-start(f32[1,256,1024]{2,1,0:T(8,128)} %param.21) | copy-start | bytes 3145732
  7.2 107.4 %copy-start.3 = (f32[1,256,64]{1,2,0:T(8,128)S(1)}, f32[1,256,64]{1,2,0:T(8,128)}, u32[]{:S(2)}) copy-start(f32[1,256,64]{1,2,0:T(8,128)} %param.22) | copy-start | bytes 196612
  7.3 46.8 %all-reduce.3.cloned.1.call-start = ((), (), s32[]{:S(2)}) async-start(), calls=%async_computation.9 | async-start | bytes 524288
  9.2 69.3 %reduce-scatter.4.cloned.1.call-start = ((), (), s32[]{:S(2)}) async-start(), calls=%async_computation.6 | async-start | bytes 327680 | tf_op jit(solution)/shard_map/reduce_scatter | solution.py:52
  10.9 101.5 %reduce-scatter.6.cloned.1.call-start = ((), (), s32[]{:S(2)}) async-start(), calls=%async_computation.7 | async-start | bytes 2621440 | tf_op jit(solution)/shard_map/reduce_scatter | solution.py:69
  11.6 218.9 %all-gather.4.cloned.1.call-start = ((), (), s32[]{:S(2)}) async-start(), calls=%async_computation.5 | async-start | bytes 4259840 | tf_op jit(solution)/shard_map/all_gather | solution.py:84
  72.4 265.5 %all-gather.6.cloned.1.call-start = ((), (), s32[]{:S(2)}) async-start(), calls=%async_computation.8 | async-start | bytes 4259840 | tf_op jit(solution)/shard_map/all_gather | solution.py:85
  114.6 41.3 %copy-start.8 = (f32[2,1024]{1,0:T(2,128)S(1)}, f32[2,1024]{1,0:T(2,128)}, u32[]{:S(2)}) copy-start(f32[2,1024]{1,0:T(2,128)} %param.23) | copy-start | bytes 24580
  114.6 41.3 %copy-start.9 = (f32[2,1024]{1,0:T(2,128)S(1)}, f32[2,1024]{1,0:T(2,128)}, u32[]{:S(2)}) copy-start(f32[2,1024]{1,0:T(2,128)} %param.24) | copy-start | bytes 24580
  116.7 5.2 %copy-start.10 = (bf16[1,2,1024]{2,1,0:T(2,128)(2,1)S(1)}, bf16[1,2,1024]{2,1,0:T(2,128)(2,1)}, u32[]{:S(2)}) copy-start(bf16[1,2,1024]{2,1,0:T(2,128)(2,1)} %param.16) | copy-start | bytes 12292
  118.3 38.9 %all-to-all-start.2 = ((bf16[4,256,1024]{2,1,0:T(8,128)(2,1)}), bf16[4,256,1024]{2,1,0:T(8,128)(2,1)S(1)}, u32[]{:S(2)}, u32[]{:S(2)}) async-start(bf16[4,256,1024]{2,1,0:T(8,128)(2,1)} %bitcast.15), calls=%async_computation.4 | async-start | bytes 4194304 | tf_op jit(solution)/shard_map/all_to_all | solution.py:9
  337.9 4.9 %copy-start.2 = (bf16[1,2048,1024]{2,1,0:T(8,128)(2,1)S(1)}, bf16[1,2048,1024]{2,1,0:T(8,128)(2,1)}, u32[]{:S(2)}) copy-start(bf16[1,2048,1024]{2,1,0:T(8,128)(2,1)} %all-gather.6.cloned.1.call-done) | copy-start | bytes 12582916
Sparse Core Ops, SparseCore 0:
  11.0 42.9 all-reduce.2
  57.1 21.2 reduce-scatter.3
  80.8 31.5 reduce-scatter.5
  114.1 116.3 all-gather.3
  232.8 105.0 all-gather.5
